TPU v7x, 128 devices: a whole 4x4x4 slice. The times are simulated.
128 devices in a mesh: blk: 2 (over z_hi), row: 64 (over x, z_lo, y, core).
Axes of the slice: x: 4, y: 4, z: 4 (z_hi: 2, z_lo: 2; z = z_hi * 2 + z_lo), core: 2. Of those that a mesh axis runs over, the one named last changes fastest.
Arguments:
- features: bfloat16 [65536, 128], P(('blk', 'row')), may hold values from -6 to 6
- tiles: bfloat16 [512, 32, 128, 128], P(('blk', 'row')), may hold values from -0.75 to 0.75
- tile_src: int32 [512, 32], P(('blk', 'row')), may hold values from 0 to 511, as said below
- tile_count: int32 [512], P(('blk', 'row')), may hold values from 1 to 32, 8448 in all
- degrees: int32 [65536], P(('blk', 'row')), may hold values from 16 to 128
- w_self: bfloat16 [128, 128], replicated, may hold values from -0.5 to 0.5
- w_neigh: bfloat16 [128, 128], replicated, may hold values from -2 to 2
- bias: float32 [128], replicated, may hold values from -3 to 3
Outputs:
- updated: bfloat16 [65536, 128], P(('blk', 'row'))
Inputs may be any that keep to these rules, and one draw needn't show every extreme that they name: `tile_src`: slots at or past tile_count of a block are unused; their tiles are arbitrary. Split the node blocks into aligned runs of 4 blocks and the destination blocks likewise: all slots of the destination blocks of one run name at most one source block of each run of source blocks.
All inputs are finite; a program needn't handle non-finite values.
Results may differ from a plain program's by a relative error of at most 0.0028.
Values may be sent and summed in bfloat16 or wider, within the bound.
A program may use at most 128 MiB of HBM per device.

v0:
```python
import jax
import jax.numpy as jnp
from jax import lax
from jax.sharding import PartitionSpec as P


def passed_along(value, axis, steps):
    count = lax.axis_size(axis)
    pairs = [(source, (source + steps) % count) for source in range(count)]
    return lax.ppermute(value, axis, pairs)


def accumulate(total, source_rows, first_block, tiles, tile_src, tile_count):
    tile_size = tiles.shape[2]
    width = source_rows.shape[1]
    held = source_rows.shape[0] // tile_size
    source_blocks = source_rows.reshape(held, tile_size, width)
    slot_total = tiles.shape[1]
    offset = tile_src - first_block
    inside = (offset >= 0) & (offset < held)
    live = inside & (jnp.arange(slot_total, dtype=jnp.int32)[None, :] < tile_count[:, None])
    picked = source_blocks[jnp.clip(offset, 0, held - 1)]
    picked = jnp.where(live[:, :, None, None], picked, jnp.zeros_like(picked))
    return total + jnp.einsum("btij,btjf->bif", tiles, picked, preferred_element_type=jnp.float32)


def per_device(features, tiles, tile_src, tile_count, degrees, w_self, w_neigh, bias):
    groups = lax.axis_size("blk")
    members = lax.axis_size("row")
    tile_size = tiles.shape[2]
    width = features.shape[1]
    group_blocks = features.shape[0] * members // tile_size
    my_group = lax.axis_index("blk")
    total = jnp.zeros((tiles.shape[0], tile_size, width), jnp.float32)
    current = lax.all_gather(features, "row", axis=0, tiled=True)
    total = accumulate(total, current, my_group * group_blocks, tiles, tile_src, tile_count)
    current = passed_along(current, "blk", 1)
    source_group = (my_group - 1) % groups
    total = accumulate(total, current, source_group * group_blocks, tiles, tile_src, tile_count)
    aggregate = total.reshape(features.shape[0], width)
    neigh_mean = (aggregate / degrees.astype(jnp.float32)[:, None]).astype(jnp.bfloat16)
    summed = jnp.dot(features, w_self, preferred_element_type=jnp.float32)
    summed = summed + jnp.dot(neigh_mean, w_neigh, preferred_element_type=jnp.float32)
    return jax.nn.relu(summed + bias[None, :]).astype(jnp.bfloat16)


def solution(mesh):
    return jax.shard_map(
        per_device,
        mesh=mesh,
        in_specs=(
            P(("blk", "row"), None),
            P(("blk", "row"), None, None, None),
            P(("blk", "row"), None),
            P(("blk", "row")),
            P(("blk", "row")),
            P(),
            P(),
            P(),
        ),
        out_specs=P(("blk", "row"), None),
        check_vma=False,
    )
```

profile of v0, /device:TPU:1, one launch (start us, length us, event | category | flops | bytes accessed | tf_op | source)
XLA Modules:
  0.0 325.5 jit_solution(3943960400396006036)
XLA Ops:
  6.5 0.0 copy-start
  6.5 0.0 all-gather.2.cloned.1.call-start
  6.5 0.7 all-gather.2.cloned.1.call-update
  7.3 115.6 %all-gather.2.cloned.1.call-done = bf16[32768,128]{1,0:T(8,128)(2,1)} async-done(((bf16[512,128]{1,0:T(8,128)(2,1)}), bf16[32768,128]{1,0:T(8,128)(2,1)}) %all-gather.2.cloned.1.call-update) | async-done | bytes 8388624 | tf_op jit(solution)/shard_map/all_gather | solution.py:35
  122.9 2.6 collective-permute-start
  125.5 0.7 compare_select_fusion
  126.2 0.1 reshape.19
  126.3 0.1 reshape.27
  126.4 0.7 convert_element_type.9
  127.1 0.8 fusion.21
  127.8 0.0 copy-done
  127.8 1.1 fusion.25
  128.9 6.4 %gather_fusion = bf16[128,128,128]{2,1,0:T(8,128)(2,1)} fusion(bf16[256,128,128]{2,1,0:T(8,128)(2,1)} %bitcast.26, s32[1024]{0:T(1024)S(1)} %pad_clamp_fusion.1), kind=kCustom, calls=%fused_computation | custom fusion | bytes 8389120 | tf_op jit(solution)/shard_map/gather | solution.py:22
  135.3 4.8 %fusion.8 = f32[4,128,128]{1,2,0:T(8,128)S(1)} fusion(bf16[4,32,128,128]{3,2,1,0:T(8,128)(2,1)} %param.9, bf16[4,32,128,128]{3,2,1,0:T(8,128)(2,1)} %bitcast.25, pred[4,32]{1,0:T(4,128)(4,1)S(1)} %get-tuple-element.6), kind=kOutput, calls=%fused_computation.10 | convolution fusion | flops 538968064 | bytes 8650880 | tf_op jit(solution)/shard_map/btij,btjf->bif/dot_general | solution.py:24
  140.1 166.3 %collective-permute-done = bf16[32768,128]{1,0:T(8,128)(2,1)} collective-permute-done((bf16[32768,128]{1,0:T(8,128)(2,1)}, bf16[32768,128]{1,0:T(8,128)(2,1)}, u32[]{:S(2)}, u32[]{:S(2)}) %collective-permute-start) | collective-permute-done | bytes 8388640 | tf_op jit(solution)/shard_map/ppermute | solution.py:10
  306.4 6.4 %gather_fusion.1 = bf16[128,128,128]{2,1,0:T(8,128)(2,1)} fusion(bf16[256,128,128]{2,1,0:T(8,128)(2,1)} %bitcast.4, s32[1024]{0:T(1024)S(1)} %pad_clamp_fusion), kind=kCustom, calls=%fused_computation.1 | custom fusion | bytes 8389120 | tf_op jit(solution)/shard_map/gather | solution.py:22
  312.8 0.0 copy-start.1
  312.8 0.0 copy-start.2
  312.8 4.8 %fusion.16 = f32[4,128,128]{1,2,0:T(8,128)S(1)} fusion(f32[4,128,128]{1,2,0:T(8,128)S(1)} %fusion.8, bf16[4,32,128,128]{3,2,1,0:T(8,128)(2,1)} %param.9, bf16[4,32,128,128]{3,2,1,0:T(8,128)(2,1)} %bitcast.24, pred[4,32]{1,0:T(4,128)(4,1)S(1)} %get-tuple-element.5), kind=kOutput, calls=%fused_computation.15 | convolution fusion | flops 539033600 | bytes 8913024 | tf_op jit(solution)/shard_map/btij,btjf->bif/dot_general | solution.py:24
  317.6 0.1 fusion.20
  317.8 0.0 copy-done.1
  317.8 0.0 copy-done.2
  317.8 0.8 fusion.19
  (2 shorter events, 0.0 us)
Async XLA Ops:
  6.5 121.3 %copy-start = (bf16[128,128]{1,0:T(8,128)(2,1)S(1)}, bf16[128,128]{1,0:T(8,128)(2,1)}, u32[]{:S(2)}) copy-start(bf16[128,128]{1,0:T(8,128)(2,1)} %param.13) | copy-start | bytes 98308
  6.5 116.3 %all-gather.2.cloned.1.call-start = ((), (), s32[]{:S(2)}) async-start(), calls=%async_computation | async-start | bytes 8519680 | tf_op jit(solution)/shard_map/all_gather | solution.py:35
  122.9 183.5 %collective-permute-start = (bf16[32768,128]{1,0:T(8,128)(2,1)}, bf16[32768,128]{1,0:T(8,128)(2,1)}, u32[]{:S(2)}, u32[]{:S(2)}) collective-permute-start(bf16[32768,128]{1,0:T(8,128)(2,1)} %all-gather.2.cloned.1.call-done), channel_id=1, source_target_pairs={{0,64},{64,0},{1,65},{65,1},{2,66},{66,2},{3,67},{67,3},{4,68},{68... | collective-permute-start | bytes 25165832 | tf_op jit(solution)/shard_map/ppermute | solution.py:10
  312.8 4.9 %copy-start.1 = (bf16[128,128]{1,0:T(8,128)(2,1)S(1)}, bf16[128,128]{1,0:T(8,128)(2,1)}, u32[]{:S(2)}) copy-start(bf16[128,128]{1,0:T(8,128)(2,1)} %param.14) | copy-start | bytes 98308
  312.8 5.0 %copy-start.2 = (f32[128]{0:T(128)S(1)}, f32[128]{0:T(128)}, u32[]{:S(2)}) copy-start(f32[128]{0:T(128)} %param.15) | copy-start | bytes 1540
Sparse Core Ops, SparseCore 0:
  9.0 113.7 all-gather.1
where the time goes:
time: 326 us; the launch traced here: 325 us
  waiting for transfers between devices  283 us (87%)
  between operations  13.4 us (4%)
  local copies, waits for them, and re-layouts  13 us (4%)
  matrix products  11.5 us (4%)
    ppermute x1, waiting for transfers between devices, passed_along(): return lax.ppermute(value, axis, pairs)  166 us
    all_gather x1, waiting for transfers between devices, per_device(): current = lax.all_gather(features, 'row', axis=0, tiled=True)  116 us
    gather x2, local copies, waits for them, and re-layouts, accumulate(): picked = source_blocks[jnp.clip(offset, 0, held - 1)]  12.8 us
    dot_general x2, matrix products, accumulate(): jnp.einsum('btij,btjf->bif', tiles, picked, preferred_element_type=jnp.fl...  9.56 us
  transfers between devices with their start and end apart: 2, of which 2 were waited for; matrix products, arithmetic and copies ran while one was open for 4% of the time, Pallas kernels for 0%

commit v1 on v0

v1 whole, which is shorter than its diff:
```python
import jax
import jax.numpy as jnp
from jax import lax
from jax.experimental import pallas as pl
from jax.experimental.pallas import tpu as pltpu
from jax.sharding import PartitionSpec as P

MESH = pl.DeviceIdType.MESH
SPLITS = ((0, 48), (48, 48), (96, 32))
ORDERS = ((0, 1, 2), (1, 2, 0), (2, 0, 1))


def place():
    group, member = lax.axis_index("blk"), lax.axis_index("row")
    x = lax.div(member, 16)
    z_low = lax.rem(lax.div(member, 8), 2)
    y = lax.rem(lax.div(member, 2), 4)
    return [x, y, group * 2 + z_low], lax.rem(member, 2)


def device(spot, core):
    x, y, z = spot
    return lax.div(z, 2), ((x * 2 + lax.rem(z, 2)) * 4 + y) * 2 + core


def shifted(spot, axis, steps):
    moved = list(spot)
    moved[axis] = lax.rem(moved[axis] + steps, 4)
    return moved


def exchange_kernel(feat, tiles, src, cnt, out0, out1, out2, tiles_out, *scratch):
    outs = (out0, out1, out2)
    held = (scratch[0:4], scratch[4:8], scratch[8:12])
    packs, relays = scratch[12:15], scratch[15:18]
    mine, table, wants = scratch[18:21]
    load_sem, tile_sem, one_recv, two_recv, held_send = scratch[21:26]
    want_send, want_recv, want_local, pack_send, out_recv, relay_recv, relay_send = scratch[26:33]

    spot, core = place()
    other = 1 - core

    loads = []
    for k, (start, rows) in enumerate(SPLITS):
        copy = pltpu.make_async_copy(feat.at[:, pl.ds(start, rows), :], held[k][0].at[0], load_sem.at[k])
        copy.start()
        loads.append(copy)
    tile_load = pltpu.make_async_copy(tiles, tiles_out, tile_sem)

    friends = [device(spot, other)]
    for axis in range(3):
        for steps in (1, 2, 3):
            for c in (core, other):
                friends.append(device(shifted(spot, axis, steps), c))
    barrier = pltpu.get_barrier_semaphore()
    for friend in friends:
        pl.semaphore_signal(barrier, inc=1, device_id=friend, device_id_type=MESH)
    pl.semaphore_wait(barrier, len(friends))

    def send(source, target, send_sem, recv_sem, where):
        copy = pltpu.make_async_remote_copy(
            src_ref=source, dst_ref=target, send_sem=send_sem, recv_sem=recv_sem,
            device_id=where, device_id_type=MESH,
        )
        copy.start()

    def arrived(ref, sem):
        pltpu.make_async_copy(ref, ref, sem).wait()

    plus = [device(shifted(spot, axis, 1), core) for axis in range(3)]
    minus = [device(shifted(spot, axis, 3), core) for axis in range(3)]
    plus_other = [device(shifted(spot, axis, 1), other) for axis in range(3)]
    minus_other = [device(shifted(spot, axis, 3), other) for axis in range(3)]

    def spread(k, d1):
        a2 = ORDERS[k][1]
        own = held[k][0].at[d1]
        send(own, held[k][3].at[d1], held_send.at[k], two_recv.at[k, d1, 0], plus[a2])
        send(own, held[k][1].at[d1], held_send.at[k], two_recv.at[k, d1, 1], minus[a2])

    def spread_on(k, d1):
        a2 = ORDERS[k][1]
        arrived(held[k][3].at[d1], two_recv.at[k, d1, 0])
        send(held[k][3].at[d1, 0:2], held[k][2].at[d1, 0:2], held_send.at[k], two_recv.at[k, d1, 2], plus[a2])
        arrived(held[k][1].at[d1], two_recv.at[k, d1, 1])
        send(held[k][1].at[d1, 2:4], held[k][2].at[d1, 2:4], held_send.at[k], two_recv.at[k, d1, 3], minus[a2])

    def select(k, d2):
        a1, a2, a3 = ORDERS[k]
        for d1 in range(4):
            group, member = device(shifted(shifted(spot, a1, d1), a2, d2), core)
            lane = group * 64 + member
            for j in range(8):
                row = j if j < 2 else 2 + k * 6 + (j - 2)
                block = held[k][d2][d1, wants[row, 0, lane]]
                if j == 0:
                    outs[k][0, d2, d1] = block
                else:
                    packs[k][j - 1, d2, d1] = block
        send(packs[k].at[0, d2], outs[k].at[1, d2], pack_send.at[k], out_recv.at[k], device(spot, other))
        send(packs[k].at[3, d2], relays[k].at[0, d2], pack_send.at[k], relay_recv.at[k, 0, d2], plus[a3])
        send(packs[k].at[4, d2], relays[k].at[1, d2], pack_send.at[k], relay_recv.at[k, 1, d2], minus[a3])
        send(packs[k].at[1, d2], outs[k].at[6, d2], pack_send.at[k], out_recv.at[k], plus[a3])
        send(packs[k].at[5, d2], outs[k].at[2, d2], pack_send.at[k], out_recv.at[k], minus[a3])
        send(packs[k].at[2, d2], outs[k].at[7, d2], pack_send.at[k], out_recv.at[k], plus_other[a3])
        send(packs[k].at[6, d2], outs[k].at[3, d2], pack_send.at[k], out_recv.at[k], minus_other[a3])

    def relay(k, d2):
        a3 = ORDERS[k][2]
        arrived(relays[k].at[0, d2], relay_recv.at[k, 0, d2])
        send(relays[k].at[0, d2], outs[k].at[4, d2], relay_send.at[k], out_recv.at[k], plus[a3])
        arrived(relays[k].at[1, d2], relay_recv.at[k, 1, d2])
        send(relays[k].at[1, d2], outs[k].at[5, d2], relay_send.at[k], out_recv.at[k], minus_other[a3])

    for k in range(3):
        loads[k].wait()
        a1 = ORDERS[k][0]
        own = held[k][0].at[0]
        send(own, held[k][0].at[3], held_send.at[k], one_recv.at[k, 0], plus[a1])
        send(own, held[k][0].at[1], held_send.at[k], one_recv.at[k, 1], minus[a1])
        spread(k, 0)
    tile_load.start()

    lanes = lax.broadcasted_iota(jnp.int32, (1, 128), 1)
    want = jnp.zeros((1, 128), jnp.int32)
    for b in range(4):
        for t in range(32):
            block = src[b, t]
            owner = jnp.where(t < cnt[b], lax.shift_right_logical(block, 2), -1)
            want = jnp.where(lanes == owner, lax.bitwise_and(block, 3), want)
    mine[...] = want
    send(mine, table.at[0], want_send, want_recv, device(spot, other))
    for k in range(3):
        a3 = ORDERS[k][2]
        for e in (1, 2, 3):
            back = shifted(spot, a3, 4 - e)
            send(mine, table.at[1 + k * 6 + e * 2 - 2], want_send, want_recv, device(back, core))
            send(mine, table.at[1 + k * 6 + e * 2 - 1], want_send, want_recv, device(back, other))

    for k in range(3):
        a1 = ORDERS[k][0]
        arrived(held[k][0].at[3], one_recv.at[k, 0])
        send(held[k][0].at[3, 0:2], held[k][0].at[2, 0:2], held_send.at[k], one_recv.at[k, 2], plus[a1])
        spread(k, 3)
        arrived(held[k][0].at[1], one_recv.at[k, 1])
        send(held[k][0].at[1, 2:4], held[k][0].at[2, 2:4], held_send.at[k], one_recv.at[k, 3], minus[a1])
        spread(k, 1)
    for k in range(3):
        spread_on(k, 0)
    for k in range(3):
        arrived(held[k][0].at[2, 0:2], one_recv.at[k, 2])
        arrived(held[k][0].at[2, 2:4], one_recv.at[k, 3])
        spread(k, 2)

    arrived(table, want_recv)
    own_row = pltpu.make_async_copy(mine, wants.at[0], want_local.at[0])
    others = pltpu.make_async_copy(table, wants.at[pl.ds(1, 19)], want_local.at[1])
    own_row.start()
    others.start()
    own_row.wait()
    others.wait()

    for k in range(3):
        select(k, 0)
        spread_on(k, 3)
        spread_on(k, 1)
    for k in range(3):
        spread_on(k, 2)
        select(k, 3)
        select(k, 1)
        relay(k, 0)
    for k in range(3):
        for d1 in range(4):
            arrived(held[k][2].at[d1, 0:2], two_recv.at[k, d1, 2])
            arrived(held[k][2].at[d1, 2:4], two_recv.at[k, d1, 3])
        select(k, 2)
    for d2 in (3, 1, 2):
        for k in range(3):
            relay(k, d2)

    for k in range(3):
        arrived(outs[k].at[pl.ds(1, 7)], out_recv.at[k])
    arrived(table, want_send)
    for k in range(3):
        arrived(packs[k], pack_send.at[k])
        arrived(relays[k], relay_send.at[k])
        sent = packs[k].at[pl.ds(0, 3), pl.ds(0, 4), pl.ds(0, 4)]
        arrived(sent, held_send.at[k])
        more = packs[k].at[0, pl.ds(0, 3), pl.ds(0, 4)]
        arrived(more, held_send.at[k])
    tile_load.wait()


def exchange(features, tiles, tile_src, tile_count):
    rows = [r for _, r in SPLITS]
    vmem = pl.BlockSpec(memory_space=pltpu.VMEM)
    smem = pl.BlockSpec(memory_space=pltpu.SMEM)
    hbm = pl.BlockSpec(memory_space=pl.ANY)
    dma = pltpu.SemaphoreType.DMA
    scratch = [pltpu.VMEM((4, 4, r, 128), jnp.bfloat16) for r in rows for _ in range(4)]
    scratch += [pltpu.VMEM((7, 4, 4, r, 128), jnp.bfloat16) for r in rows]
    scratch += [pltpu.VMEM((2, 4, 4, r, 128), jnp.bfloat16) for r in rows]
    scratch += [pltpu.VMEM((1, 128), jnp.int32), pltpu.VMEM((19, 1, 128), jnp.int32), pltpu.SMEM((20, 1, 128), jnp.int32)]
    scratch += [dma((3,)), dma, dma((3, 4)), dma((3, 4, 4)), dma((3,))]
    scratch += [dma, dma, dma((2,)), dma((3,)), dma((3,)), dma((3, 2, 4)), dma((3,))]
    shapes = [jax.ShapeDtypeStruct((8, 4, 4, r, 128), jnp.bfloat16) for r in rows]
    shapes.append(jax.ShapeDtypeStruct(tiles.shape, tiles.dtype))
    return pl.pallas_call(
        exchange_kernel,
        out_shape=shapes,
        in_specs=[hbm, hbm, smem, smem],
        out_specs=[vmem] * 4,
        scratch_shapes=scratch,
        compiler_params=pltpu.CompilerParams(collective_id=0, has_side_effects=True, vmem_limit_bytes=60 << 20),
        name="exchange",
    )(features, tiles, tile_src, tile_count)


def combine_kernel(src, cnt, f0, f1, f2, tiles, feat, deg, w_self, w_neigh, bias, out):
    spot, core = place()
    x, y, z = spot

    def one_block(b, carry):
        live = cnt[b]
        total = jnp.zeros((128, 128), jnp.float32)
        for pair in range(16):
            blocks, sides = [], []
            for t in (2 * pair, 2 * pair + 1):
                owner = lax.shift_right_logical(src[b, t], 2)
                rc = lax.bitwise_xor(lax.bitwise_and(owner, 1), core)
                sy = lax.bitwise_and(lax.shift_right_logical(owner, 1), 3)
                sx = lax.bitwise_and(lax.shift_right_logical(owner, 4), 3)
                sz = lax.bitwise_and(lax.shift_right_logical(owner, 3), 1) + 2 * lax.shift_right_logical(owner, 6)
                rx, ry, rz = (lax.bitwise_and(s - m, 3) for s, m in ((sx, x), (sy, y), (sz, z)))
                block = jnp.concatenate([
                    f0[((rz * 2 + rc) * 4 + ry) * 4 + rx],
                    f1[((rx * 2 + rc) * 4 + rz) * 4 + ry],
                    f2[((ry * 2 + rc) * 4 + rx) * 4 + rz],
                ], axis=0)
                blocks.append(jnp.where(t < live, block, jnp.zeros_like(block)))
                sides.append(tiles[b, t])
            total = total + jnp.dot(
                jnp.concatenate(sides, axis=1), jnp.concatenate(blocks, axis=0),
                preferred_element_type=jnp.float32,
            )
        rows = pl.ds(pl.multiple_of(b * 128, 128), 128)
        degrees = jnp.broadcast_to(deg[pl.ds(b, 1), :].astype(jnp.float32), (128, 128)).T
        mean = (total / degrees).astype(jnp.bfloat16)
        summed = jnp.dot(feat[rows, :], w_self[...], preferred_element_type=jnp.float32)
        summed = summed + jnp.dot(mean, w_neigh[...], preferred_element_type=jnp.float32)
        out[rows, :] = jnp.maximum(summed + bias[...], 0.0).astype(jnp.bfloat16)
        return carry

    lax.fori_loop(0, 4, one_block, 0)


def combine(picked, tiles, features, tile_src, tile_count, degrees, w_self, w_neigh, bias):
    vmem = pl.BlockSpec(memory_space=pltpu.VMEM)
    smem = pl.BlockSpec(memory_space=pltpu.SMEM)
    return pl.pallas_call(
        combine_kernel,
        out_shape=jax.ShapeDtypeStruct(features.shape, jnp.bfloat16),
        in_specs=[smem, smem] + [vmem] * 9,
        out_specs=vmem,
        compiler_params=pltpu.CompilerParams(vmem_limit_bytes=60 << 20),
        name="combine",
    )(tile_src, tile_count, *picked, tiles, features, degrees, w_self, w_neigh, bias)


def per_device(features, tiles, tile_src, tile_count, degrees, w_self, w_neigh, bias):
    *picked, held_tiles = exchange(features.reshape(4, 128, 128), tiles, tile_src, tile_count)
    picked = [p.reshape(128, p.shape[3], 128) for p in picked]
    return combine(
        picked, held_tiles, features, tile_src, tile_count,
        degrees.reshape(4, 128), w_self, w_neigh, bias.reshape(1, 128),
    )


def solution(mesh):
    return jax.shard_map(
        per_device,
        mesh=mesh,
        in_specs=(
            P(("blk", "row"), None),
            P(("blk", "row"), None, None, None),
            P(("blk", "row"), None),
            P(("blk", "row")),
            P(("blk", "row")),
            P(),
            P(),
            P(),
        ),
        out_specs=P(("blk", "row"), None),
        check_vma=False,
    )
```

time: 326 us -> 52.2 us (0.16)
  waiting for transfers between devices: 283 us -> 0 us
  Pallas kernels: 0 us -> 52.1 us
  between operations: 13.4 us -> 0.01 us
  local copies, waits for them, and re-layouts: 13 us -> 0 us
  matrix products: 11.5 us -> 0 us
    ppermute x1 -> x0, waiting for transfers between devices: 166 us -> none  [passed_along(): return lax.ppermute(value, axis, pairs)]
    all_gather x1 -> x0, waiting for transfers between devices: 116 us -> none  [per_device(): current = lax.all_gather(features, 'row', axis=0, tiled=True)]
    pallas_call x0 -> x2, Pallas kernels: none -> 52.1 us  [the longest x1 44.8 us: exchange(): pl.pallas_call(exchange_kernel, out_shape=shapes, in_specs=[hbm, hbm, sme...]
    gather x2 -> x0, local copies, waits for them, and re-layouts: 12.8 us -> none  [accumulate(): picked = source_blocks[jnp.clip(offset, 0, held - 1)]]
    dot_general x4 -> x0, matrix products: 11.5 us -> none  [the longest x2 9.56 us: accumulate(): jnp.einsum('btij,btjf->bif', tiles, picked, preferred_element_type=jnp.fl...]
  transfers between devices with their start and end apart: 2 -> 0, of which waited for: 2 -> 0; matrix products, arithmetic and copies ran while one was open for 4% -> 0% of each run, Pallas kernels for 0% -> 0%
where the time goes in v1:
time: 52.2 us; the launch traced here: 52.1 us
  Pallas kernels  52.1 us (100%)
    pallas_call x1, Pallas kernels, exchange(): pl.pallas_call(exchange_kernel, out_shape=shapes, in_specs=[hbm, hbm, sme...  44.8 us
    pallas_call x1, Pallas kernels, combine(): pl.pallas_call(combine_kernel, out_shape=jax.ShapeDtypeStruct(features.sh...  7.27 us

profile of v1, /device:TPU:1, one launch (start us, length us, event | category | flops | bytes accessed | tf_op | source)
XLA Modules:
  0.0 52.1 jit_solution(4889272860730189445)
XLA Ops:
  0.0 44.8 %exchange.1 = (bf16[8,4,4,48,128]{4,3,2,1,0:T(8,128)(2,1)}, bf16[8,4,4,48,128]{4,3,2,1,0:T(8,128)(2,1)}, bf16[8,4,4,32,128]{4,3,2,1,0:T(8,128)(2,1)}, bf16[4,32,128,128]{3,2,1,0:T(8,128)(2,1)}) custom-call(bf16[4,128,128]{2,1,0:T(8,128)(2,1)} %bitcast.9, bf16[4,32,128,128]{3,2,1,0:T(8,128)(2,1)} %tiles.1, s32[4,32]{1,0:T(4,128)} %src.3, s32[4]{0:T(128)} %cnt.3), custom_call_target="tpu_custom_call" | custom-call | tf_op jit(solution)/shard_map/exchange/pallas_call | solution.py:208
  44.8 7.3 %combine.1 = bf16[512,128]{1,0:T(8,128)(2,1)} custom-call(s32[4,32]{1,0:T(4,128)} %src.3, s32[4]{0:T(128)} %cnt.3, bf16[128,48,128]{2,1,0:T(8,128)(2,1)} %bitcast.6, bf16[128,48,128]{2,1,0:T(8,128)(2,1)} %bitcast.7, bf16[128,32,128]{2,1,0:T(8,128)(2,1)} %bitcast.8, bf16[4,32,128,128]{3,2,1,0:T(8,128)(2,1)} %get-tuple-element.12.tiles, ...), custom_call_target="tpu_custom_call" | custom-call | tf_op jit(solution)/shard_map/combine/pallas_call | solution.py:260

commit v2 on v1

v2 whole, which is shorter than its diff:
```python
import jax
import jax.numpy as jnp
from jax import lax
from jax.experimental import pallas as pl
from jax.experimental.pallas import tpu as pltpu
from jax.sharding import PartitionSpec as P

MESH = pl.DeviceIdType.MESH
VMEM_BYTES = 66_800_000
SPLITS = ((0, 48), (48, 48), (96, 32))
ORDERS = ((0, 1, 2), (1, 2, 0), (2, 0, 1))


def place():
    group, member = lax.axis_index("blk"), lax.axis_index("row")
    x = lax.div(member, 16)
    z_low = lax.rem(lax.div(member, 8), 2)
    y = lax.rem(lax.div(member, 2), 4)
    return [x, y, group * 2 + z_low], lax.rem(member, 2)


def device(spot, core):
    x, y, z = spot
    return lax.div(z, 2), ((x * 2 + lax.rem(z, 2)) * 4 + y) * 2 + core


def shifted(spot, axis, steps):
    moved = list(spot)
    moved[axis] = lax.rem(moved[axis] + steps, 4)
    return moved


def layer_kernel(feat, tiles, src_hbm, cnt_hbm, deg_hbm, self_hbm, neigh_hbm, bias_hbm, out, *scratch):
    held = (scratch[0:4], scratch[4:8], scratch[8:12])
    packs, relays, outs = scratch[12:15], scratch[15:18], scratch[18:21]
    mine, table, wants, src, cnt, src_vec, spots_vec, spots = scratch[21:29]
    feat_vec, tiles_vec, deg, w_self, w_neigh, bias, base = scratch[29:36]
    load_sem, one_recv, two_recv, held_send = scratch[36:40]
    want_send, want_recv, want_local, pack_send, out_recv, relay_recv, relay_send = scratch[40:47]

    spot, core = place()
    other = 1 - core

    def load(source, target, at):
        copy = pltpu.make_async_copy(source, target, load_sem.at[at])
        copy.start()
        return copy

    loads = [
        load(feat.at[:, pl.ds(start, rows), :], held[k][0].at[0], k)
        for k, (start, rows) in enumerate(SPLITS)
    ]
    table_loads = [load(src_hbm, src, 3), load(cnt_hbm, cnt, 4), load(src_hbm, src_vec, 5)]

    friends = [device(spot, other)]
    for axis in range(3):
        for steps in (1, 2, 3):
            for c in (core, other):
                friends.append(device(shifted(spot, axis, steps), c))
    barrier = pltpu.get_barrier_semaphore()
    for friend in friends:
        pl.semaphore_signal(barrier, inc=1, device_id=friend, device_id_type=MESH)
    pl.semaphore_wait(barrier, len(friends))

    def send(source, target, send_sem, recv_sem, where):
        copy = pltpu.make_async_remote_copy(
            src_ref=source, dst_ref=target, send_sem=send_sem, recv_sem=recv_sem,
            device_id=where, device_id_type=MESH,
        )
        copy.start()

    def arrived(ref, sem):
        pltpu.make_async_copy(ref, ref, sem).wait()

    plus = [device(shifted(spot, axis, 1), core) for axis in range(3)]
    minus = [device(shifted(spot, axis, 3), core) for axis in range(3)]
    plus_other = [device(shifted(spot, axis, 1), other) for axis in range(3)]
    minus_other = [device(shifted(spot, axis, 3), other) for axis in range(3)]

    def spread(k, d1):
        a2 = ORDERS[k][1]
        own = held[k][0].at[d1]
        send(own, held[k][3].at[d1], held_send.at[k], two_recv.at[k, d1, 0], plus[a2])
        send(own, held[k][1].at[d1], held_send.at[k], two_recv.at[k, d1, 1], minus[a2])

    def spread_on(k, d1):
        a2 = ORDERS[k][1]
        arrived(held[k][3].at[d1], two_recv.at[k, d1, 0])
        send(held[k][3].at[d1, 0:2], held[k][2].at[d1, 0:2], held_send.at[k], two_recv.at[k, d1, 2], plus[a2])
        arrived(held[k][1].at[d1], two_recv.at[k, d1, 1])
        send(held[k][1].at[d1, 2:4], held[k][2].at[d1, 2:4], held_send.at[k], two_recv.at[k, d1, 3], minus[a2])

    def part(k, source, d2):
        return outs[k].at[pl.ds(source * 16 + d2 * 4, 4)]

    def select(k, d2):
        a1, a2, a3 = ORDERS[k]
        for d1 in range(4):
            group, member = device(shifted(shifted(spot, a1, d1), a2, d2), core)
            lane = group * 64 + member
            for j in range(8):
                row = j if j < 2 else 2 + k * 6 + (j - 2)
                block = held[k][d2][d1, wants[row, 0, lane]]
                if j == 0:
                    outs[k][d2 * 4 + d1] = block
                else:
                    packs[k][j - 1, d2, d1] = block
        send(packs[k].at[0, d2], part(k, 1, d2), pack_send.at[k], out_recv.at[k], device(spot, other))
        send(packs[k].at[3, d2], relays[k].at[0, d2], pack_send.at[k], relay_recv.at[k, 0, d2], plus[a3])
        send(packs[k].at[4, d2], relays[k].at[1, d2], pack_send.at[k], relay_recv.at[k, 1, d2], minus[a3])
        send(packs[k].at[1, d2], part(k, 6, d2), pack_send.at[k], out_recv.at[k], plus[a3])
        send(packs[k].at[5, d2], part(k, 2, d2), pack_send.at[k], out_recv.at[k], minus[a3])
        send(packs[k].at[2, d2], part(k, 7, d2), pack_send.at[k], out_recv.at[k], plus_other[a3])
        send(packs[k].at[6, d2], part(k, 3, d2), pack_send.at[k], out_recv.at[k], minus_other[a3])

    def relay(k, d2):
        a3 = ORDERS[k][2]
        arrived(relays[k].at[0, d2], relay_recv.at[k, 0, d2])
        send(relays[k].at[0, d2], part(k, 4, d2), relay_send.at[k], out_recv.at[k], plus[a3])
        arrived(relays[k].at[1, d2], relay_recv.at[k, 1, d2])
        send(relays[k].at[1, d2], part(k, 5, d2), relay_send.at[k], out_recv.at[k], minus_other[a3])

    for k in range(3):
        loads[k].wait()
        a1 = ORDERS[k][0]
        own = held[k][0].at[0]
        send(own, held[k][0].at[3], held_send.at[k], one_recv.at[k, 0], plus[a1])
        send(own, held[k][0].at[1], held_send.at[k], one_recv.at[k, 1], minus[a1])
        spread(k, 0)
    late_loads = [
        load(feat, feat_vec, 6), load(deg_hbm, deg, 7), load(self_hbm, w_self, 8),
        load(neigh_hbm, w_neigh, 9), load(bias_hbm, bias, 10), load(tiles, tiles_vec, 11),
    ]
    for copy in table_loads:
        copy.wait()

    lanes = lax.broadcasted_iota(jnp.int32, (1, 128), 1)
    want = jnp.zeros((1, 128), jnp.int32)
    for b in range(4):
        for t in range(32):
            block = src[b, t]
            owner = jnp.where(t < cnt[b], lax.shift_right_logical(block, 2), -1)
            want = jnp.where(lanes == owner, lax.bitwise_and(block, 3), want)
    mine[...] = want
    send(mine, table.at[0], want_send, want_recv, device(spot, other))
    for k in range(3):
        a3 = ORDERS[k][2]
        for e in (1, 2, 3):
            back = shifted(spot, a3, 4 - e)
            send(mine, table.at[1 + k * 6 + e * 2 - 2], want_send, want_recv, device(back, core))
            send(mine, table.at[1 + k * 6 + e * 2 - 1], want_send, want_recv, device(back, other))

    owner = lax.shift_right_logical(src_vec[...], 2)
    rc = lax.bitwise_xor(lax.bitwise_and(owner, 1), core)
    sy = lax.bitwise_and(lax.shift_right_logical(owner, 1), 3)
    sx = lax.bitwise_and(lax.shift_right_logical(owner, 4), 3)
    sz = lax.bitwise_and(lax.shift_right_logical(owner, 3), 1) + 2 * lax.shift_right_logical(owner, 6)
    rx, ry, rz = (lax.bitwise_and(s - m, 3) for s, m in zip((sx, sy, sz), spot))
    slots = lax.broadcasted_iota(jnp.int32, (4, 32), 1)
    which = lax.broadcasted_iota(jnp.int32, (4, 32), 0)
    counts = jnp.where(which == 0, cnt[0], jnp.where(which == 1, cnt[1], jnp.where(which == 2, cnt[2], cnt[3])))
    for k, (d1, d2, d3) in enumerate(((rx, ry, rz), (ry, rz, rx), (rz, rx, ry))):
        spots_vec[k] = jnp.where(slots < counts, ((d3 * 2 + rc) * 4 + d2) * 4 + d1, 128)
    spots_copy = pltpu.make_async_copy(spots_vec, spots, want_local.at[2])
    spots_copy.start()
    for k, (_, rows) in enumerate(SPLITS):
        outs[k][128] = jnp.zeros((rows, 128), jnp.bfloat16)

    for k in range(3):
        a1 = ORDERS[k][0]
        arrived(held[k][0].at[3], one_recv.at[k, 0])
        send(held[k][0].at[3, 0:2], held[k][0].at[2, 0:2], held_send.at[k], one_recv.at[k, 2], plus[a1])
        spread(k, 3)
        arrived(held[k][0].at[1], one_recv.at[k, 1])
        send(held[k][0].at[1, 2:4], held[k][0].at[2, 2:4], held_send.at[k], one_recv.at[k, 3], minus[a1])
        spread(k, 1)
    for k in range(3):
        spread_on(k, 0)
    for k in range(3):
        arrived(held[k][0].at[2, 0:2], one_recv.at[k, 2])
        arrived(held[k][0].at[2, 2:4], one_recv.at[k, 3])
        spread(k, 2)

    arrived(table, want_recv)
    own_row = pltpu.make_async_copy(mine, wants.at[0], want_local.at[0])
    others = pltpu.make_async_copy(table, wants.at[pl.ds(1, 19)], want_local.at[1])
    own_row.start()
    others.start()
    own_row.wait()
    others.wait()

    for k in range(3):
        select(k, 0)
        spread_on(k, 3)
        spread_on(k, 1)
    for k in range(3):
        spread_on(k, 2)
        select(k, 3)
        select(k, 1)
        relay(k, 0)
    for k in range(3):
        for d1 in range(4):
            arrived(held[k][2].at[d1, 0:2], two_recv.at[k, d1, 2])
            arrived(held[k][2].at[d1, 2:4], two_recv.at[k, d1, 3])
        select(k, 2)
    for k in range(3):
        relay(k, 3)
        relay(k, 1)

    for copy in late_loads:
        copy.wait()
    for b in range(4):
        base[b] = jnp.dot(feat_vec[b], w_self[...], preferred_element_type=jnp.float32) + bias[...]

    for k in range(3):
        relay(k, 2)
    spots_copy.wait()
    for k in range(3):
        arrived(outs[k].at[pl.ds(16, 112)], out_recv.at[k])

    def one_block(b, carry):
        total = jnp.zeros((128, 128), jnp.float32)
        for pair in range(16):
            slot_pair = (2 * pair, 2 * pair + 1)
            blocks = [outs[k][spots[k, b, t]] for t in slot_pair for k in range(3)]
            total = total + jnp.dot(
                jnp.concatenate([tiles_vec[b, t] for t in slot_pair], axis=1),
                jnp.concatenate(blocks, axis=0),
                preferred_element_type=jnp.float32,
            )
        degrees = jnp.broadcast_to(deg[pl.ds(b, 1), :].astype(jnp.float32), (128, 128)).T
        mean = (total / degrees).astype(jnp.bfloat16)
        summed = base[b] + jnp.dot(mean, w_neigh[...], preferred_element_type=jnp.float32)
        out[b] = jnp.maximum(summed, 0.0).astype(jnp.bfloat16)
        return carry

    lax.fori_loop(0, 4, one_block, 0)

    arrived(table, want_send)
    for k in range(3):
        arrived(packs[k], pack_send.at[k])
        arrived(relays[k], relay_send.at[k])
        sent = packs[k].at[pl.ds(0, 3), pl.ds(0, 4), pl.ds(0, 4)]
        arrived(sent, held_send.at[k])
        more = packs[k].at[0, pl.ds(0, 3), pl.ds(0, 4)]
        arrived(more, held_send.at[k])


def per_device(features, tiles, tile_src, tile_count, degrees, w_self, w_neigh, bias):
    rows = [r for _, r in SPLITS]
    dma = pltpu.SemaphoreType.DMA
    wide, whole, real = jnp.bfloat16, jnp.int32, jnp.float32
    scratch = [pltpu.VMEM((4, 4, r, 128), wide) for r in rows for _ in range(4)]
    scratch += [pltpu.VMEM((7, 4, 4, r, 128), wide) for r in rows]
    scratch += [pltpu.VMEM((2, 4, 4, r, 128), wide) for r in rows]
    scratch += [pltpu.VMEM((129, r, 128), wide) for r in rows]
    scratch += [pltpu.VMEM((1, 128), whole), pltpu.VMEM((19, 1, 128), whole), pltpu.SMEM((20, 1, 128), whole)]
    scratch += [pltpu.SMEM((4, 32), whole), pltpu.SMEM((4,), whole), pltpu.VMEM((4, 32), whole)]
    scratch += [pltpu.VMEM((3, 4, 32), whole), pltpu.SMEM((3, 4, 32), whole)]
    scratch += [pltpu.VMEM((4, 128, 128), wide), pltpu.VMEM((4, 32, 128, 128), wide), pltpu.VMEM((4, 128), whole)]
    scratch += [pltpu.VMEM((128, 128), wide), pltpu.VMEM((128, 128), wide), pltpu.VMEM((1, 128), real)]
    scratch += [pltpu.VMEM((4, 128, 128), real)]
    scratch += [dma((12,)), dma((3, 4)), dma((3, 4, 4)), dma((3,))]
    scratch += [dma, dma, dma((3,)), dma((3,)), dma((3,)), dma((3, 2, 4)), dma((3,))]
    updated = pl.pallas_call(
        layer_kernel,
        out_shape=pltpu.VMEM((4, 128, 128), jnp.bfloat16),
        in_specs=[pl.BlockSpec(memory_space=pl.ANY)] * 8,
        out_specs=pl.BlockSpec(memory_space=pltpu.VMEM),
        scratch_shapes=scratch,
        compiler_params=pltpu.CompilerParams(
            collective_id=0, has_side_effects=True, vmem_limit_bytes=VMEM_BYTES
        ),
        name="layer",
    )(
        features.reshape(4, 128, 128), tiles, tile_src, tile_count,
        degrees.reshape(4, 128), w_self, w_neigh, bias.reshape(1, 128),
    )
    return updated.reshape(features.shape)


def solution(mesh):
    return jax.shard_map(
        per_device,
        mesh=mesh,
        in_specs=(
            P(("blk", "row"), None),
            P(("blk", "row"), None, None, None),
            P(("blk", "row"), None),
            P(("blk", "row")),
            P(("blk", "row")),
            P(),
            P(),
            P(),
        ),
        out_specs=P(("blk", "row"), None),
        check_vma=False,
    )
```

time: 52.2 us -> 43.9 us (0.84)
  Pallas kernels: 52.1 us -> 43.2 us
  local copies, waits for them, and re-layouts: 0 us -> 0.66 us
    pallas_call x2 -> x1, Pallas kernels: 52.1 us -> 43.2 us  [per_device(): pl.pallas_call(layer_kernel, out_shape=pltpu.VMEM((4, 128, 128), jnp.bflo...]
    unnamed x0 -> x1, local copies, waits for them, and re-layouts: none -> 0.66 us
where the time goes in v2:
time: 43.9 us; the launch traced here: 43.8 us
  Pallas kernels  43.2 us (98%)
  local copies, waits for them, and re-layouts  0.66 us (2%)
    pallas_call x1, Pallas kernels, per_device(): pl.pallas_call(layer_kernel, out_shape=pltpu.VMEM((4, 128, 128), jnp.bflo...  43.2 us

profile of v2, /device:TPU:1, one launch (start us, length us, event | category | flops | bytes accessed | tf_op | source)
XLA Modules:
  0.0 43.8 jit_solution(10984082146028391019)
XLA Ops:
  0.0 43.2 %layer.1 = bf16[4,128,128]{2,1,0:T(8,128)(2,1)S(1)} custom-call(bf16[4,128,128]{2,1,0:T(8,128)(2,1)} %bitcast.5, bf16[4,32,128,128]{3,2,1,0:T(8,128)(2,1)} %tiles.1, s32[4,32]{1,0:T(4,128)} %src_hbm.1, s32[4]{0:T(128)} %cnt_hbm.1, s32[4,128]{1,0:T(4,128)} %bitcast.6, bf16[128,128]{1,0:T(8,128)(2,1)} %self_hbm.1, bf16[128,128]{1,0:T(8,128)(2,1)} %neigh_hbm.1, ...), custom_call_target="tpu_custom_call" | custom-call | tf_op jit(solution)/shard_map/layer/pallas_call | solution.py:265
  43.2 0.7 %copy.10 = bf16[512,128]{1,0:T(8,128)(2,1)} copy(bf16[512,128]{1,0:T(8,128)(2,1)S(1)} %bitcast.4) | data formatting | bytes 262144

commit v3 on v0

v3 whole, which is shorter than its diff:
```python
import jax
import jax.numpy as jnp
from jax import lax
from jax.experimental import pallas as pl
from jax.experimental.pallas import tpu as pltpu
from jax.sharding import PartitionSpec as P

MESH = pl.DeviceIdType.MESH
VMEM_BYTES = 66_800_000
COLOURS = ((0, 48, (0, 1, 2), 0), (48, 48, (1, 2, 0), 1), (96, 32, (2, 0, 1), 0))
INNER = (
    ((0, 0, 0), -1, 0),
    ((1, 0, 0), 0, 1),
    ((0, 1, 0), 0, 1),
    ((0, 0, 3), 0, 1),
    ((1, 3, 0), 1, 2),
    ((1, 0, 3), 1, 2),
    ((3, 1, 0), 2, 2),
    ((0, 1, 1), 2, 2),
    ((0, 3, 3), 3, 2),
    ((2, 3, 0), 4, 3),
    ((1, 1, 3), 5, 3),
    ((1, 0, 2), 5, 3),
    ((3, 1, 1), 7, 3),
    ((0, 2, 1), 7, 3),
    ((2, 3, 1), 9, 4),
    ((1, 2, 3), 10, 4),
    ((3, 1, 2), 12, 4),
    ((3, 2, 2), 16, 5),
)
LEAVES = (
    ((0, 3, 0), 0), ((3, 0, 0), 0), ((0, 0, 1), 0), ((2, 0, 0), 1),
    ((1, 0, 1), 1), ((0, 1, 3), 2), ((1, 1, 0), 2), ((0, 2, 0), 2),
    ((3, 0, 3), 3), ((0, 0, 2), 3), ((1, 2, 0), 4), ((1, 3, 3), 4),
    ((1, 3, 1), 4), ((2, 0, 3), 5), ((2, 1, 0), 6), ((3, 2, 0), 6),
    ((3, 1, 3), 6), ((1, 1, 1), 7), ((0, 1, 2), 7), ((3, 3, 3), 8),
    ((0, 2, 3), 8), ((0, 3, 2), 8), ((2, 2, 0), 9), ((3, 3, 0), 9),
    ((2, 3, 3), 9), ((2, 1, 3), 10), ((1, 1, 2), 10), ((1, 3, 2), 11),
    ((2, 0, 2), 11), ((2, 1, 1), 12), ((3, 0, 1), 12), ((0, 3, 1), 13),
    ((1, 2, 1), 13), ((3, 2, 1), 13), ((0, 2, 2), 13), ((2, 2, 1), 14),
    ((2, 0, 1), 14), ((3, 3, 1), 14), ((2, 3, 2), 14), ((2, 2, 3), 15),
    ((1, 2, 2), 15), ((3, 0, 2), 16), ((2, 1, 2), 16), ((3, 2, 3), 17),
    ((3, 3, 2), 17), ((2, 2, 2), 17),
)
HELD = len(INNER)
PICKED = 128 - HELD


def place():
    group, member = lax.axis_index("blk"), lax.axis_index("row")
    x = lax.div(member, 16)
    z_low = lax.rem(lax.div(member, 8), 2)
    y = lax.rem(lax.div(member, 2), 4)
    return [x, y, group * 2 + z_low], lax.rem(member, 2)


def device(spot, core):
    x, y, z = spot
    return lax.div(z, 2), ((x * 2 + lax.rem(z, 2)) * 4 + y) * 2 + core


def either(flip, first, second):
    same = isinstance(first, int) and first == second
    return first if same else first + flip * (second - first)


def edge(offset, parent):
    from_parent = [(o - p) % 4 for o, p in zip(offset, INNER[parent][0])]
    axis = [a for a in range(3) if from_parent[a]][0]
    return axis, from_parent[axis] // 2


def layer_kernel(feat, tiles, src_hbm, cnt_hbm, deg_hbm, self_hbm, neigh_hbm, bias_hbm, out, *scratch):
    colours = range(len(COLOURS))
    refs = list(scratch)
    held = [[refs.pop(0) for _ in range(HELD)] for _ in colours]
    packs = [refs.pop(0) for _ in colours]
    picked, mine, table, wants, src, cnt, src_vec, spots_vec, spots = refs[:9]
    feat_vec, tiles_vec, deg, w_self, w_neigh, bias, base = refs[9:16]
    load_sem, held_recv, held_send, want_send, want_recv, want_local, pack_send, picked_recv = refs[16:]

    spot, core = place()
    other = 1 - core

    def load(source, target, at):
        copy = pltpu.make_async_copy(source, target, load_sem.at[at])
        copy.start()
        return copy

    own_loads = [
        load(feat.at[:, pl.ds(COLOURS[k][0], COLOURS[k][1]), :], held[k][0], 9 + k) for k in colours
    ]
    table_loads = [load(src_hbm, src, 0), load(cnt_hbm, cnt, 1), load(src_hbm, src_vec, 2)]

    near = {}
    for axis in range(3):
        for down in (0, 1):
            moved = list(spot)
            moved[axis] = lax.rem(moved[axis] + (3 if down else 1), 4)
            for c, at in enumerate((core, other)):
                near[axis, down, c] = device(moved, at)
    partner = device(spot, other)
    friends = [partner] + list(near.values())
    barrier = pltpu.get_barrier_semaphore()
    for friend in friends:
        pl.semaphore_signal(barrier, inc=1, device_id=friend, device_id_type=MESH)
    pl.semaphore_wait(barrier, len(friends))

    def send(source, target, send_sem, recv_sem, where):
        pltpu.make_async_remote_copy(
            src_ref=source, dst_ref=target, send_sem=send_sem, recv_sem=recv_sem,
            device_id=where, device_id_type=MESH,
        ).start()

    def arrived(ref, sem):
        pltpu.make_async_copy(ref, ref, sem).wait()

    flips = [core if mirror == 0 else other for _, _, _, mirror in COLOURS]

    def toward(k, axis, down, c):
        real = COLOURS[k][2][axis]
        up, low = near[real, down, c], near[real, 1 - down, c]
        return either(flips[k], up[0], low[0]), either(flips[k], up[1], low[1])

    def laid(k, offset):
        real = [0, 0, 0]
        for axis in range(3):
            real[COLOURS[k][2][axis]] = offset[axis]
        return real

    def number(k, offset, c):
        x, y, z = laid(k, offset)
        mx, my, mz = (-x % 4, -y % 4, -z % 4)
        return either(flips[k], ((x * 4 + y) * 4 + z) * 2 + c, ((mx * 4 + my) * 4 + mz) * 2 + c)

    lane_parts = {}

    def lane_part(k, axis, step):
        key = (COLOURS[k][3], axis, step)
        if key not in lane_parts:
            at = lax.rem(spot[axis] + either(flips[k], -step % 4, step), 4)
            lane_parts[key] = (
                at * 16 if axis == 0 else at * 2 if axis == 1 else lax.div(at, 2) * 64 + lax.rem(at, 2) * 8
            )
        return lane_parts[key]

    def pass_on(k, i):
        for j, (offset, parent, _) in enumerate(INNER):
            if parent == i:
                send(held[k][i], held[k][j], held_send.at[k], held_recv.at[k, j], toward(k, *edge(offset, i), 0))

    waiting = []

    def flush():
        for args in waiting:
            send(*args)
        waiting.clear()

    def select(k, i):
        start, rows = COLOURS[k][:2]
        mine_offset = INNER[i][0]
        steps = laid(k, mine_offset)
        lane = lane_part(k, 0, steps[0]) + lane_part(k, 1, steps[1]) + lane_part(k, 2, steps[2]) + core
        picked[number(k, mine_offset, 0), pl.ds(start, rows), :] = held[k][i][wants[0, 0, lane]]
        packs[k][i] = held[k][i][wants[1, 0, lane]]
        sends = [(i, mine_offset, 1, partner)]
        for l, (offset, parent) in enumerate(LEAVES):
            if parent != i:
                continue
            axis, down = edge(offset, i)
            real = COLOURS[k][2][axis]
            for c in (0, 1):
                row = 2 + (real * 2 + either(flips[k], down, 1 - down)) * 2 + c
                at = HELD + 2 * l + c
                packs[k][at] = held[k][i][wants[row, 0, lane]]
                sends.append((at, offset, c, toward(k, axis, down, c)))
        flush()
        for at, offset, c, where in sends:
            target = picked.at[number(k, offset, c), pl.ds(start, rows), :]
            waiting.append((packs[k].at[at], target, pack_send.at[k], picked_recv.at[k], where))

    for k in colours:
        own_loads[k].wait()
        pass_on(k, 0)
    late_loads = [
        load(feat, feat_vec, 3), load(deg_hbm, deg, 4), load(self_hbm, w_self, 5),
        load(neigh_hbm, w_neigh, 6), load(bias_hbm, bias, 7), load(tiles, tiles_vec, 8),
    ]
    for copy in table_loads:
        copy.wait()

    lanes = lax.broadcasted_iota(jnp.int32, (1, 128), 1)
    want = jnp.zeros((1, 128), jnp.int32)
    for b in range(4):
        for t in range(32):
            block = src[b, t]
            owner = jnp.where(t < cnt[b], lax.shift_right_logical(block, 2), -1)
            want = jnp.where(lanes == owner, lax.bitwise_and(block, 3), want)
    mine[...] = want

    owner = lax.shift_right_logical(src_vec[...], 2)
    rc = lax.bitwise_xor(lax.bitwise_and(owner, 1), core)
    sy = lax.bitwise_and(lax.shift_right_logical(owner, 1), 3)
    sx = lax.bitwise_and(lax.shift_right_logical(owner, 4), 3)
    sz = lax.bitwise_and(lax.shift_right_logical(owner, 3), 1) + 2 * lax.shift_right_logical(owner, 6)
    vx, vy, vz = (lax.bitwise_and(m - s, 3) for s, m in zip((sx, sy, sz), spot))
    slots = lax.broadcasted_iota(jnp.int32, (4, 32), 1)
    which = lax.broadcasted_iota(jnp.int32, (4, 32), 0)
    counts = jnp.where(which == 0, cnt[0], jnp.where(which == 1, cnt[1], jnp.where(which == 2, cnt[2], cnt[3])))
    spots_vec[...] = jnp.where(slots < counts, ((vx * 4 + vy) * 4 + vz) * 2 + rc, 128)

    send(mine, table.at[0], want_send, want_recv, partner)
    for (axis, down, c), where in near.items():
        send(mine, table.at[1 + (axis * 2 + 1 - down) * 2 + c], want_send, want_recv, where)
    spots_copy = pltpu.make_async_copy(spots_vec, spots, want_local.at[2])
    spots_copy.start()
    own_row = pltpu.make_async_copy(mine, wants.at[0], want_local.at[0])
    own_row.start()
    picked[128] = jnp.zeros((128, 128), jnp.bfloat16)

    levels = [[i for i, node in enumerate(INNER) if node[2] == level] for level in range(INNER[-1][2] + 1)]

    def step(level):
        for i in levels[level]:
            for k in colours:
                arrived(held[k][i], held_recv.at[k, i])
                pass_on(k, i)

    step(1)
    arrived(table, want_recv)
    others = pltpu.make_async_copy(table, wants.at[pl.ds(1, 13)], want_local.at[1])
    others.start()
    own_row.wait()
    others.wait()
    for k in colours:
        select(k, 0)
    for level in range(1, len(levels)):
        for i in levels[level]:
            for k in colours:
                select(k, i)
        flush()
        if level + 1 < len(levels):
            step(level + 1)

    for copy in late_loads:
        copy.wait()
    for b in range(4):
        base[b] = jnp.dot(feat_vec[b], w_self[...], preferred_element_type=jnp.float32) + bias[...]
    spots_copy.wait()
    for k in colours:
        start, rows = COLOURS[k][:2]
        arrived(picked.at[pl.ds(0, PICKED), pl.ds(start, rows), :], picked_recv.at[k])

    def one_block(b, carry):
        total = jnp.zeros((128, 128), jnp.float32)
        for pair in range(16):
            slot_pair = (2 * pair, 2 * pair + 1)
            total = total + jnp.dot(
                jnp.concatenate([tiles_vec[b, t] for t in slot_pair], axis=1),
                jnp.concatenate([picked[spots[b, t]] for t in slot_pair], axis=0),
                preferred_element_type=jnp.float32,
            )
        degrees = jnp.broadcast_to(deg[pl.ds(b, 1), :].astype(jnp.float32), (128, 128)).T
        mean = (total / degrees).astype(jnp.bfloat16)
        summed = base[b] + jnp.dot(mean, w_neigh[...], preferred_element_type=jnp.float32)
        out[b] = jnp.maximum(summed, 0.0).astype(jnp.bfloat16)
        return carry

    lax.fori_loop(0, 4, one_block, 0)

    arrived(table, want_send)
    for k in colours:
        start, rows = COLOURS[k][:2]
        arrived(packs[k], pack_send.at[k])
        arrived(picked.at[pl.ds(0, 4 * (HELD - 1)), pl.ds(start, rows), :], held_send.at[k])


def per_device(features, tiles, tile_src, tile_count, degrees, w_self, w_neigh, bias):
    rows = [colour[1] for colour in COLOURS]
    n = len(rows)
    dma = pltpu.SemaphoreType.DMA
    wide, whole, real = jnp.bfloat16, jnp.int32, jnp.float32
    scratch = [pltpu.VMEM((4, r, 128), wide) for r in rows for _ in range(HELD)]
    scratch += [pltpu.VMEM((HELD + 2 * len(LEAVES), r, 128), wide) for r in rows]
    scratch += [pltpu.VMEM((129, 128, 128), wide)]
    scratch += [pltpu.VMEM((1, 128), whole), pltpu.VMEM((13, 1, 128), whole), pltpu.SMEM((14, 1, 128), whole)]
    scratch += [pltpu.SMEM((4, 32), whole), pltpu.SMEM((4,), whole), pltpu.VMEM((4, 32), whole)]
    scratch += [pltpu.VMEM((4, 32), whole), pltpu.SMEM((4, 32), whole)]
    scratch += [pltpu.VMEM((4, 128, 128), wide), pltpu.VMEM((4, 32, 128, 128), wide), pltpu.VMEM((4, 128), whole)]
    scratch += [pltpu.VMEM((128, 128), wide), pltpu.VMEM((128, 128), wide), pltpu.VMEM((1, 128), real)]
    scratch += [pltpu.VMEM((4, 128, 128), real)]
    scratch += [dma((9 + n,)), dma((n, HELD)), dma((n,)), dma, dma, dma((3,)), dma((n,)), dma((n,))]
    updated = pl.pallas_call(
        layer_kernel,
        out_shape=pltpu.VMEM((4, 128, 128), jnp.bfloat16),
        in_specs=[pl.BlockSpec(memory_space=pl.ANY)] * 8,
        out_specs=pl.BlockSpec(memory_space=pltpu.VMEM),
        scratch_shapes=scratch,
        compiler_params=pltpu.CompilerParams(
            collective_id=0, has_side_effects=True, vmem_limit_bytes=VMEM_BYTES
        ),
        name="layer",
    )(
        features.reshape(4, 128, 128), tiles, tile_src, tile_count,
        degrees.reshape(4, 128), w_self, w_neigh, bias.reshape(1, 128),
    )
    return updated.reshape(features.shape)


def solution(mesh):
    return jax.shard_map(
        per_device,
        mesh=mesh,
        in_specs=(
            P(("blk", "row"), None),
            P(("blk", "row"), None, None, None),
            P(("blk", "row"), None),
            P(("blk", "row")),
            P(("blk", "row")),
            P(),
            P(),
            P(),
        ),
        out_specs=P(("blk", "row"), None),
        check_vma=False,
    )
```

time: 326 us -> 37.2 us (0.11)
  waiting for transfers between devices: 283 us -> 0 us
  Pallas kernels: 0 us -> 36.4 us
  between operations: 13.4 us -> 0.01 us
  local copies, waits for them, and re-layouts: 13 us -> 0.66 us
  matrix products: 11.5 us -> 0 us
    ppermute x1 -> x0, waiting for transfers between devices: 166 us -> none  [passed_along(): return lax.ppermute(value, axis, pairs)]
    all_gather x1 -> x0, waiting for transfers between devices: 116 us -> none  [per_device(): current = lax.all_gather(features, 'row', axis=0, tiled=True)]
    pallas_call x0 -> x1, Pallas kernels: none -> 36.4 us  [per_device(): pl.pallas_call(layer_kernel, out_shape=pltpu.VMEM((4, 128, 128), jnp.bflo...]
    gather x2 -> x0, local copies, waits for them, and re-layouts: 12.8 us -> none  [accumulate(): picked = source_blocks[jnp.clip(offset, 0, held - 1)]]
    dot_general x4 -> x0, matrix products: 11.5 us -> none  [the longest x2 9.56 us: accumulate(): jnp.einsum('btij,btjf->bif', tiles, picked, preferred_element_type=jnp.fl...]
  transfers between devices with their start and end apart: 2 -> 0, of which waited for: 2 -> 0; matrix products, arithmetic and copies ran while one was open for 4% -> 0% of each run, Pallas kernels for 0% -> 0%
where the time goes in v3:
time: 37.2 us; the launch traced here: 37.1 us
  Pallas kernels  36.4 us (98%)
  local copies, waits for them, and re-layouts  0.66 us (2%)
    pallas_call x1, Pallas kernels, per_device(): pl.pallas_call(layer_kernel, out_shape=pltpu.VMEM((4, 128, 128), jnp.bflo...  36.4 us

profile of v3, /device:TPU:1, one launch (start us, length us, event | category | flops | bytes accessed | tf_op | source)
XLA Modules:
  0.0 37.1 jit_solution(16813467739777730822)
XLA Ops:
  0.0 36.4 %layer.1 = bf16[4,128,128]{2,1,0:T(8,128)(2,1)S(1)} custom-call(bf16[4,128,128]{2,1,0:T(8,128)(2,1)} %bitcast.5, bf16[4,32,128,128]{3,2,1,0:T(8,128)(2,1)} %tiles.1, s32[4,32]{1,0:T(4,128)} %src_hbm.1, s32[4]{0:T(128)} %cnt_hbm.1, s32[4,128]{1,0:T(4,128)} %bitcast.6, bf16[128,128]{1,0:T(8,128)(2,1)} %self_hbm.1, bf16[128,128]{1,0:T(8,128)(2,1)} %neigh_hbm.1, ...), custom_call_target="tpu_custom_call" | custom-call | tf_op jit(solution)/shard_map/layer/pallas_call | solution.py:293
  36.4 0.7 %copy.10 = bf16[512,128]{1,0:T(8,128)(2,1)} copy(bf16[512,128]{1,0:T(8,128)(2,1)S(1)} %bitcast.4) | data formatting | bytes 262144
